TPU v7x, 512 devices: a whole 4x8x8 slice. The times are simulated.
512 devices in a mesh: seq: 64 (over z, x, y_lo), tp: 8 (over y_hi, core).
Axes of the slice: x: 4, y: 8 (y_hi: 4, y_lo: 2; y = y_hi * 2 + y_lo), z: 8, core: 2. Of those that a mesh axis runs over, the one named last changes fastest.
Arguments:
- tokens: bfloat16 [16384, 4096], P('seq', 'tp'), may hold values from -6 to 6
- x_weight: bfloat16 [4096, 8192], P('seq', 'tp'), may hold values from -0.09375 to 0.09375
- bc_weight: bfloat16 [4096, 256], P('seq', 'tp'), may hold values from -0.09375 to 0.09375
- dt_weight: bfloat16 [4096, 128], P('seq', 'tp'), may hold values from -0.09375 to 0.09375
- conv_x: float32 [4, 8192], P(None, 'tp'), may hold values from -2.5 to 2.5
- conv_bc: float32 [4, 256], replicated, may hold values from -2.5 to 2.5
- dt_bias: float32 [128], P('tp'), may hold values from -3 to 0
- decay_rate: float32 [128], P('tp'), may hold values from 6.1035155e-07 to 0.07
- d_skip: float32 [128], P('tp'), may hold values from 0.5 to 2
- norm_gain: float32 [8192], P('tp'), may hold values from 0.5 to 1.5
- initial_state: float32 [128, 64, 128], P('tp'), may hold values from -16 to 16
- steer: float32 [8192], P('tp'), may hold values from -6 to 6
Outputs:
- steered: bfloat16 [16384, 8192], P('seq', 'tp')
All inputs are finite; a program needn't handle non-finite values.
Results may differ from a plain program's by a relative error of at most 0.0055.
Values may be sent and summed in bfloat16 or wider, within the bound.
No kernel may reach another device: no remote copies, remote signals or barrier semaphores. Data moves between devices by JAX's collectives and lax.ppermute only.
A program may use at most 64 MiB of HBM per device.

v0:
```python
import jax
import jax.numpy as jnp
from jax import lax
from jax.sharding import PartitionSpec as P

N = 128
GROUP = 128
EPSILON = 1e-05


def passed_along(value, axis, steps):
    count = lax.axis_size(axis)
    first, last = (max(0, -steps), min(count, count - steps))
    return lax.ppermute(value, axis, [(source, source + steps) for source in range(first, last)])


def prefix(x, axis, combine, identity):
    count, mine = (lax.axis_size(axis), lax.axis_index(axis))
    everything = jax.tree.map(
        lambda part, kind: lax.all_gather(part.astype(kind), axis), x, (jnp.bfloat16, jnp.bfloat16)
    )
    start = jax.tree.map(
        lambda part, zero: jnp.broadcast_to(jnp.asarray(zero, part.dtype), part.shape), x, identity
    )

    def turn(k, before):
        reached = k < mine
        new = combine(
            before, jax.tree.map(lambda part, own: part[k].astype(own.dtype), everything, x)
        )
        return jax.tree.map(lambda a, b: jnp.where(reached, a, b), new, before)

    return lax.fori_loop(0, count, turn, start)


def convolve(extended, kernel):
    kernel_rows = kernel.shape[0]
    length = extended.shape[0] - kernel_rows + 1
    summed = kernel[0] * extended[0:length].astype(jnp.float32)
    for offset in range(1, kernel_rows):
        summed = summed + kernel[offset] * extended[offset : offset + length].astype(jnp.float32)
    return jax.nn.silu(summed).astype(jnp.bfloat16)


def block_update(carry_state, inputs):
    x_block, b_block, c_block, a_block, dt_block = inputs
    length = a_block.shape[0]
    cumulative = jnp.cumsum(a_block, axis=0)
    scores = jnp.dot(c_block, b_block.T, preferred_element_type=jnp.float32)
    causal = lax.broadcasted_iota(jnp.int32, (length, length), 0) >= lax.broadcasted_iota(
        jnp.int32, (length, length), 1
    )
    differ = cumulative[:, None, :] - cumulative[None, :, :]
    decays = jnp.where(causal[:, :, None], jnp.exp(jnp.where(causal[:, :, None], differ, 0.0)), 0.0)
    mixing = (scores[:, :, None] * decays * dt_block[None, :, :]).astype(jnp.bfloat16)
    inside = jnp.einsum("tsh,shp->thp", mixing, x_block, preferred_element_type=jnp.float32)
    carried_in = jnp.einsum(
        "tn,hpn->thp", c_block.astype(jnp.float32), carry_state, precision=lax.Precision.HIGHEST
    )
    outputs = inside + jnp.exp(cumulative)[:, :, None] * carried_in
    to_end = jnp.exp(cumulative[-1][None, :] - cumulative) * dt_block
    scaled = (x_block.astype(jnp.float32) * to_end[:, :, None]).astype(jnp.bfloat16)
    added_state = jnp.einsum("shp,sn->hpn", scaled, b_block, preferred_element_type=jnp.float32)
    return (jnp.exp(cumulative[-1])[:, None, None] * carry_state + added_state, outputs)


def combine_carry(earlier, later):
    return (earlier[0] * later[0], later[0][:, None, None] * earlier[1] + later[1])


def per_device(
    tokens,
    x_weight,
    bc_weight,
    dt_weight,
    conv_x,
    conv_bc,
    dt_bias,
    decay_rate,
    d_skip,
    norm_gain,
    initial_state,
    steer,
):
    features = lax.all_gather(tokens, "tp", axis=1, tiled=True)
    rim_rows = conv_x.shape[0] - 1
    local_tokens = features.shape[0]
    head_count = dt_weight.shape[1]
    channels = x_weight.shape[1]
    head_size = channels // head_count
    bc_panel = lax.all_gather(bc_weight, "tp", axis=1, tiled=True)
    x_sums = jnp.dot(
        features,
        lax.all_gather(x_weight, "seq", axis=0, tiled=True),
        preferred_element_type=jnp.float32,
    )
    bc_sums = jnp.dot(
        features,
        lax.all_gather(bc_panel, "seq", axis=0, tiled=True),
        preferred_element_type=jnp.float32,
    )
    dt_sums = jnp.dot(
        features,
        lax.all_gather(dt_weight, "seq", axis=0, tiled=True),
        preferred_element_type=jnp.float32,
    )
    x_pre = x_sums.astype(jnp.bfloat16)
    bc_pre = bc_sums.astype(jnp.bfloat16)
    joined = jnp.concatenate(
        [x_pre[local_tokens - rim_rows :], bc_pre[local_tokens - rim_rows :]], 1
    )
    arrived = passed_along(joined, "seq", 1)
    x_extended = jnp.concatenate([arrived[:, :channels], x_pre], 0)
    bc_extended = jnp.concatenate([arrived[:, channels:], bc_pre], 0)
    x_conv = convolve(x_extended, conv_x)
    bc_conv = convolve(bc_extended, conv_bc)
    b_values = bc_conv[:, :N]
    c_values = bc_conv[:, N:]
    step_size = jax.nn.softplus(dt_sums + dt_bias[None, :])
    log_decay = -step_size * decay_rate[None, :]
    blocks = local_tokens // GROUP
    x_heads = x_conv.reshape(local_tokens, head_count, head_size)
    inputs = (
        x_heads.reshape(blocks, GROUP, head_count, head_size),
        b_values.reshape(blocks, GROUP, N),
        c_values.reshape(blocks, GROUP, N),
        log_decay.reshape(blocks, GROUP, head_count),
        step_size.reshape(blocks, GROUP, head_count),
    )
    zero_state = jnp.zeros((head_count, head_size, N), jnp.float32)
    local_state, local_out = lax.scan(block_update, zero_state, inputs)
    running = jnp.cumsum(log_decay, axis=0)
    local_decay = jnp.exp(running[-1])
    identity = (
        jnp.ones((head_count,), jnp.float32),
        jnp.zeros((head_count, head_size, N), jnp.float32),
    )
    prefix_decay, prefix_state = prefix((local_decay, local_state), "seq", combine_carry, identity)
    entering = prefix_decay[:, None, None] * initial_state + prefix_state
    from_entering = jnp.einsum(
        "tn,hpn->thp", c_values.astype(jnp.float32), entering, precision=lax.Precision.HIGHEST
    )
    outputs = (
        local_out.reshape(local_tokens, head_count, head_size)
        + jnp.exp(running)[:, :, None] * from_entering
        + d_skip[None, :, None] * x_heads.astype(jnp.float32)
    )
    mean_square = jnp.mean(outputs * outputs, axis=-1, keepdims=True)
    normed = (outputs * lax.rsqrt(mean_square + EPSILON)).reshape(
        local_tokens, channels
    ) * norm_gain[None, :]
    partial_dot = jnp.sum(normed * steer[None, :], axis=1)
    total_dot = lax.psum(partial_dot, "tp")
    penalty = total_dot / jnp.sqrt(jnp.float32(channels * lax.axis_size("tp")))
    return (normed - penalty[:, None] * steer[None, :]).astype(jnp.bfloat16)


def solution(mesh):
    placed = (
        P("seq", "tp"),
        P("seq", "tp"),
        P("seq", "tp"),
        P("seq", "tp"),
        P(None, "tp"),
        P(),
        P("tp"),
        P("tp"),
        P("tp"),
        P("tp"),
        P("tp", None, None),
        P("tp"),
    )
    return jax.shard_map(
        per_device, mesh=mesh, in_specs=placed, out_specs=P("seq", "tp"), check_vma=False
    )
```

profile of v0, /device:TPU:1, one launch (start us, length us, event | category | flops | bytes accessed | tf_op | source)
XLA Modules:
  0.0 1208.3 jit_solution(8973249411349206538)
XLA Ops:
  7.3 21.4 %all_gather.28 = bf16[64,256]{0,1:T(8,128)(2,1)S(1)} all-gather(bf16[64,32]{0,1:T(8,128)(2,1)} %param.18), channel_id=1, replica_groups=mesh['seq'=64,'tp'=8] {'tp'}, dimensions={1}, use_global_device_ids=true | all-gather | bytes 36864 | tf_op jit(solution)/shard_map/all_gather | solution.py:91
  30.3 134.9 %all-gather.1 = bf16[64,64,16]{1,2,0:T(8,128)(2,1)S(1)} all-gather(bf16[1,64,16]{1,2,0:T(8,128)(2,1)} %bitcast.146), channel_id=1, replica_groups=mesh['seq'=64,'tp'=8] {'seq'}, dimensions={0}, use_global_device_ids=true | all-gather | bytes 133120 | tf_op jit(solution)/shard_map/all_gather | solution.py:104
  167.3 147.8 %all-gather.12.cloned.1.call-done = bf16[4096,256]{1,0:T(8,128)(2,1)} async-done(((bf16[64,256]{1,0:T(8,128)(2,1)}), bf16[4096,256]{1,0:T(8,128)(2,1)}) %all-gather.12.cloned.1.call-update) | async-done | bytes 2097168 | tf_op jit(solution)/shard_map/all_gather | solution.py:99
  315.1 2.9 convolution_convert_fusion.1
  318.1 328.3 %all-gather.10.cloned.1.call-done = bf16[4096,1024]{1,0:T(8,128)(2,1)} async-done(((bf16[64,1024]{1,0:T(8,128)(2,1)}), bf16[4096,1024]{1,0:T(8,128)(2,1)}) %all-gather.10.cloned.1.call-update) | async-done | bytes 8388624 | tf_op jit(solution)/shard_map/all_gather | solution.py:94
  646.4 5.7 convolution_convert_fusion
  652.2 1.9 collective-permute-start
  657.4 29.9 %while.29 = (s32[]{:T(128)}, f32[16,64,128]{2,1,0:T(8,128)S(1)}, f32[2,128,16,64]{1,0,3,2:T(2,128)}, f32[2,128,16]{2,1,0:T(8,128)S(1)}, bf16[2,128,16,64]{1,3,2,...) while((s32[]{:T(128)}, f32[16,64,128]{2,1,0:T(8,128)S(1)}, ...), condition=%wide.region_2.3_spmd.clone, body=%wide.region_0.2_spmd.clone.sunk | while | flops 275662848 | bytes 5196752 | solution.py:131
  659.0 13.0 %dynamic_update_slice.6 = f32[2,128,16,64]{1,0,3,2:T(2,128)} dynamic-update-slice(f32[2,128,16,64]{1,0,3,2:T(2,128)} %get-tuple-element.433, f32[1,128,16,64]{1,0,3,2:T(1,128)S(1)} %bitcast.133, s32[]{:T(128)} %get-tuple-element.431, s32[]{:T(128)} %constant.65.clone.1..sunk, s32[]{:T(128)} %constant.65.clone.1..sunk, s32[]{:T(128)} %constant.65.clone.1..sunk) | dynamic-update-slice | bytes 1048580 | tf_op jit(solution)/shard_map/while/body/jit(dynamic_update_index_in_dim)/dynamic_update_slice | solution.py:131
  674.0 13.0 %dynamic_update_slice.6 = f32[2,128,16,64]{1,0,3,2:T(2,128)} dynamic-update-slice(f32[2,128,16,64]{1,0,3,2:T(2,128)} %get-tuple-element.433, f32[1,128,16,64]{1,0,3,2:T(1,128)S(1)} %bitcast.133, s32[]{:T(128)} %get-tuple-element.431, s32[]{:T(128)} %constant.65.clone.1..sunk, s32[]{:T(128)} %constant.65.clone.1..sunk, s32[]{:T(128)} %constant.65.clone.1..sunk) | dynamic-update-slice | bytes 1048580 | tf_op jit(solution)/shard_map/while/body/jit(dynamic_update_index_in_dim)/dynamic_update_slice | solution.py:131
  689.4 133.3 %all-gather.2 = bf16[64,1,16]{2,1,0:T(2,128)(2,1)S(1)} all-gather(bf16[1,1,16]{2,1,0:T(2,128)(2,1)S(1)} %bitcast.151), channel_id=1, replica_groups=mesh['seq'=64,'tp'=8] {'seq'}, dimensions={0}, use_global_device_ids=true | all-gather | bytes 2080 | tf_op jit(solution)/shard_map/all_gather | solution.py:20
  823.0 2.1 reshape.112
  825.1 286.8 %all-gather.14.cloned.1.call-done = bf16[1024,64,128]{2,1,0:T(8,128)(2,1)} async-done(((bf16[16,64,128]{2,1,0:T(8,128)(2,1)}), bf16[1024,64,128]{2,1,0:T(8,128)(2,1)}) %all-gather.14.cloned.1.call-update) | async-done | bytes 16777232 | tf_op jit(solution)/shard_map/all_gather | solution.py:20
  1111.9 73.0 %while.30 = (s32[]{:T(128)}, f32[16]{0:T(128)S(1)}, f32[16,64,128]{2,1,0:T(8,128)S(1)}, s32[]{:T(128)}, bf16[64,16]{1,0:T(8,128)(2,1)S(1)}, /*index=5*/bf16[64,16,64,128]{3,2,1,0:T(8,128)(2,1)}, s32[]{:T(128)}, s32[]{:T(128)}) while((s32[]{:T(128)}, f32[16]{0:T(128)S(1)}, f32[16,64,128]{2,1,0:T(8,128)S(1)}, s32[]{:T(128)}, ...), condition=%wide.region_6.7_spmd.clone, body=%wide.region_5.6_spmd.clone.sunk | while | flops 655428 | bytes 1311123 | solution.py:33
  1111.9 1.1 fusion.85
  1113.1 1.1 fusion.85
  1115.4 1.1 fusion.85
  1116.5 1.1 fusion.85
  1118.8 1.1 fusion.85
  1119.9 1.1 fusion.85
  1123.4 1.1 fusion.85
  1126.8 1.1 fusion.85
  1130.2 1.1 fusion.85
  1186.3 14.5 %psum.7 = f32[256]{0:T(256)S(1)} all-reduce(f32[256]{0:T(256)S(1)} %get-tuple-element.306), channel_id=1, replica_groups=mesh['seq'=64,'tp'=8] {'tp'}, use_global_device_ids=true, to_apply=%region_9.10 | all-reduce | flops 256 | bytes 2048 | tf_op jit(solution)/shard_map/psum | solution.py:153
  (212 shorter events, 77.4 us)
Async XLA Ops:
  6.5 160.7 %all-gather.8.cloned.1.call-start = ((), (), s32[]{:S(2)}) async-start(), calls=%async_computation | async-start | bytes 2359296 | tf_op jit(solution)/shard_map/all_gather | solution.py:85
  7.3 307.9 %all-gather.12.cloned.1.call-start = ((), (), s32[]{:S(2)}) async-start(), calls=%async_computation.2 | async-start | bytes 2129920 | tf_op jit(solution)/shard_map/all_gather | solution.py:99
  29.5 616.9 %all-gather.10.cloned.1.call-start = ((), (), s32[]{:S(2)}) async-start(), calls=%async_computation.1 | async-start | bytes 8519680 | tf_op jit(solution)/shard_map/all_gather | solution.py:94
  30.2 1081.7 %all-gather.14.cloned.1.call-start = ((), (), s32[]{:S(2)}) async-start(), calls=%async_computation.3 | async-start | bytes 17039360 | tf_op jit(solution)/shard_map/all_gather | solution.py:20
  167.3 479.1 %copy-start = (bf16[256,4096]{1,0:T(8,128)(2,1)S(1)}, bf16[256,4096]{1,0:T(8,128)(2,1)}, u32[]{:S(2)}) copy-start(bf16[256,4096]{1,0:T(8,128)(2,1)} %all-gather.8.cloned.1.call-done) | copy-start | bytes 6291460
  318.1 336.0 %copy-start.4 = (f32[16]{0:T(128)S(1)}, f32[16]{0:T(128)}, u32[]{:S(2)}) copy-start(f32[16]{0:T(128)} %param.23) | copy-start | bytes 196
  318.1 336.0 %copy-start.6 = (f32[16]{0:T(128)S(1)}, f32[16]{0:T(128)}, u32[]{:S(2)}) copy-start(f32[16]{0:T(128)} %param.22) | copy-start | bytes 196
  652.2 2.8 collective-permute-start
  657.4 30.8 %copy-start.3 = (f32[1024]{0:T(1024)S(1)}, f32[1024]{0:T(1024)}, u32[]{:S(2)}) copy-start(f32[1024]{0:T(1024)} %param.25) | copy-start | bytes 12292
  657.4 30.8 %copy-start.2 = (f32[1024]{0:T(1024)S(1)}, f32[1024]{0:T(1024)}, u32[]{:S(2)}) copy-start(f32[1024]{0:T(1024)} %param.27) | copy-start | bytes 12292
  1111.9 73.0 %copy-start.1 = (f32[16,64,128]{2,1,0:T(8,128)S(1)}, f32[16,64,128]{2,1,0:T(8,128)}, u32[]{:S(2)}) copy-start(f32[16,64,128]{2,1,0:T(8,128)} %param.26) | copy-start | bytes 1572868
  1111.9 73.0 %copy-start.5 = (f32[16]{0:T(128)S(1)}, f32[16]{0:T(128)}, u32[]{:S(2)}) copy-start(f32[16]{0:T(128)} %param.24) | copy-start | bytes 196
Sparse Core Ops, SparseCore 0:
  9.5 44.7 all-gather.7
  56.3 258.7 all-gather.11
  317.2 329.1 all-gather.9
  688.3 423.5 all-gather.13
where the time goes:
time: 1210 us
  waiting for transfers between devices  764 us (63%)
  blocking collectives  304 us (25%)
  other arithmetic  75.7 us (6%)
  local copies, waits for them, and re-layouts  34.1 us (3%)
  between operations  13.4 us (1%)
  matrix products  12.8 us (1%)
    all_gather x1, waiting for transfers between devices, per_device(): lax.all_gather(x_weight, 'seq', axis=0, tiled=True)  328 us
    all_gather x1, waiting for transfers between devices, prefix(): lax.all_gather(part.astype(kind), axis)  287 us
    all_gather x1, waiting for transfers between devices, per_device(): lax.all_gather(bc_panel, 'seq', axis=0, tiled=True)  148 us
    all_gather x1, blocking collectives, per_device(): lax.all_gather(dt_weight, 'seq', axis=0, tiled=True)  135 us
    all_gather x1, blocking collectives, prefix(): lax.all_gather(part.astype(kind), axis)  133 us
    select_n x128, other arithmetic, turn(): return jax.tree.map(lambda a, b: jnp.where(reached, a, b), new, before)  71.3 us
    dynamic_update_slice x2, local copies, waits for them, and re-layouts, per_device(): local_state, local_out = lax.scan(block_update, zero_state, inputs)  26.1 us
  transfers between devices with their start and end apart: 5, of which 3 were waited for; matrix products, arithmetic and copies ran while one was open for 1% of the time, Pallas kernels for 0%

commit v1 on v0

--- a/solution.py
+++ b/solution.py
@@ -1,3 +1,4 @@
+import functools
 import jax
 import jax.numpy as jnp
 from jax import lax
@@ -6,6 +7,15 @@
 N = 128
 GROUP = 128
 EPSILON = 1e-05
+
+
+def _enter_tables(unit, named_axis):
+    r2 = jnp.stack(lax.axis_size(named_axis) * [unit], axis=0)
+    y2 = lax.all_to_all(r2, named_axis, 0, 0)
+    return jnp.concatenate(y2, 0)
+
+
+table_follow = functools.partial(_enter_tables, named_axis="seq")
 
 
 def passed_along(value, axis, steps):
@@ -89,11 +99,7 @@
     channels = x_weight.shape[1]
     head_size = channels // head_count
     bc_panel = lax.all_gather(bc_weight, "tp", axis=1, tiled=True)
-    x_sums = jnp.dot(
-        features,
-        lax.all_gather(x_weight, "seq", axis=0, tiled=True),
-        preferred_element_type=jnp.float32,
-    )
+    x_sums = jnp.dot(features, table_follow(x_weight), preferred_element_type=jnp.float32)
     bc_sums = jnp.dot(
         features,
         lax.all_gather(bc_panel, "seq", axis=0, tiled=True),

time: 1210 us -> 1030 us (0.85)
  waiting for transfers between devices: 764 us -> 422 us
  blocking collectives: 304 us -> 441 us
  starting transfers between devices: 1.98 us -> 17.9 us
    all_gather x1 -> x0, waiting for transfers between devices: 328 us -> none  [per_device(): lax.all_gather(x_weight, 'seq', axis=0, tiled=True)]
    all_gather x1, blocking collectives: 21.4 us -> 158 us  [per_device(): bc_panel = lax.all_gather(bc_weight, 'tp', axis=1, tiled=True)]
    all_to_all x0 -> x1, starting transfers between devices: none -> 15.8 us  [_enter_tables(): y2 = lax.all_to_all(r2, named_axis, 0, 0)]
    all_gather x1, waiting for transfers between devices: 148 us -> 134 us  [per_device(): lax.all_gather(bc_panel, 'seq', axis=0, tiled=True)]
  transfers between devices with their start and end apart: 5 -> 5, of which waited for: 3 -> 2; matrix products, arithmetic and copies ran while one was open for 1% -> 1% of each run, Pallas kernels for 0% -> 0%
where the time goes in v1:
time: 1030 us; the launch traced here: 1020 us
  blocking collectives  441 us (43%)
  waiting for transfers between devices  422 us (41%)
  other arithmetic  75.7 us (7%)
  local copies, waits for them, and re-layouts  37.6 us (4%)
  starting transfers between devices  17.9 us (2%)
  between operations  13.5 us (1%)
  matrix products  12.8 us (1%)
    all_gather x1, waiting for transfers between devices, prefix(): lax.all_gather(part.astype(kind), axis)  286 us
    all_gather x1, blocking collectives, per_device(): bc_panel = lax.all_gather(bc_weight, 'tp', axis=1, tiled=True)  158 us
    all_gather x1, blocking collectives, per_device(): lax.all_gather(dt_weight, 'seq', axis=0, tiled=True)  137 us
    all_gather x1, waiting for transfers between devices, per_device(): lax.all_gather(bc_panel, 'seq', axis=0, tiled=True)  134 us
    all_gather x1, blocking collectives, prefix(): lax.all_gather(part.astype(kind), axis)  132 us
    select_n x128, other arithmetic, turn(): return jax.tree.map(lambda a, b: jnp.where(reached, a, b), new, before)  71.3 us
    dynamic_update_slice x2, local copies, waits for them, and re-layouts, per_device(): local_state, local_out = lax.scan(block_update, zero_state, inputs)  26.1 us
  transfers between devices with their start and end apart: 5, of which 2 were waited for; matrix products, arithmetic and copies ran while one was open for 1% of the time, Pallas kernels for 0%

profile of v1, /device:TPU:1, one launch (start us, length us, event | category | flops | bytes accessed | tf_op | source)
XLA Modules:
  0.0 1022.0 jit_solution(7644363658215580892)
XLA Ops:
  6.5 5.2 stack.2
  11.8 15.8 %all-to-all-start = ((bf16[64,64,1024]{2,1,0:T(8,128)(2,1)}), bf16[64,64,1024]{2,1,0:T(8,128)(2,1)}, u32[]{:S(2)}, u32[]{:S(2)}) async-start(bf16[64,64,1024]{2,1,0:T(8,128)(2,1)} %stack.2), calls=%async_computation | async-start | bytes 16777216 | tf_op jit(solution)/shard_map/all_to_all | solution.py:14
  28.3 157.8 %all_gather.24 = bf16[64,256]{0,1:T(8,128)(2,1)S(1)} all-gather(bf16[64,32]{0,1:T(8,128)(2,1)S(1)} %copy-done.5), channel_id=1, replica_groups=mesh['seq'=64,'tp'=8] {'tp'}, dimensions={1}, use_global_device_ids=true | all-gather | bytes 36864 | tf_op jit(solution)/shard_map/all_gather | solution.py:101
  187.0 136.7 %all-gather.1 = bf16[64,64,16]{1,2,0:T(8,128)(2,1)S(1)} all-gather(bf16[1,64,16]{1,2,0:T(8,128)(2,1)S(1)} %bitcast.147), channel_id=1, replica_groups=mesh['seq'=64,'tp'=8] {'seq'}, dimensions={0}, use_global_device_ids=true | all-gather | bytes 133120 | tf_op jit(solution)/shard_map/all_gather | solution.py:110
  324.1 134.5 %all-gather.9.cloned.1.call-done = bf16[4096,256]{1,0:T(8,128)(2,1)} async-done(((bf16[64,256]{1,0:T(8,128)(2,1)}), bf16[4096,256]{1,0:T(8,128)(2,1)}) %all-gather.9.cloned.1.call-update) | async-done | bytes 2097168 | tf_op jit(solution)/shard_map/all_gather | solution.py:105
  458.6 2.9 convolution_convert_fusion.1
  461.6 5.7 convolution_convert_fusion
  467.3 2.0 collective-permute-start
  472.7 29.9 %while.29 = (s32[]{:T(128)}, f32[16,64,128]{2,1,0:T(8,128)S(1)}, f32[2,128,16,64]{1,0,3,2:T(2,128)}, f32[2,128,16]{2,1,0:T(8,128)S(1)}, bf16[2,128,16,64]{1,3,2,...) while((s32[]{:T(128)}, f32[16,64,128]{2,1,0:T(8,128)S(1)}, ...), condition=%wide.region_2.3_spmd.clone, body=%wide.region_0.2_spmd.clone.sunk | while | flops 275662848 | bytes 5196752 | solution.py:137
  474.3 13.1 %dynamic_update_slice.6 = f32[2,128,16,64]{1,0,3,2:T(2,128)} dynamic-update-slice(f32[2,128,16,64]{1,0,3,2:T(2,128)} %get-tuple-element.433, f32[1,128,16,64]{1,0,3,2:T(1,128)S(1)} %bitcast.134, s32[]{:T(128)} %get-tuple-element.431, s32[]{:T(128)} %constant.65.clone.1..sunk, s32[]{:T(128)} %constant.65.clone.1..sunk, s32[]{:T(128)} %constant.65.clone.1..sunk) | dynamic-update-slice | bytes 1048580 | tf_op jit(solution)/shard_map/while/body/jit(dynamic_update_index_in_dim)/dynamic_update_slice | solution.py:137
  489.3 13.1 %dynamic_update_slice.6 = f32[2,128,16,64]{1,0,3,2:T(2,128)} dynamic-update-slice(f32[2,128,16,64]{1,0,3,2:T(2,128)} %get-tuple-element.433, f32[1,128,16,64]{1,0,3,2:T(1,128)S(1)} %bitcast.134, s32[]{:T(128)} %get-tuple-element.431, s32[]{:T(128)} %constant.65.clone.1..sunk, s32[]{:T(128)} %constant.65.clone.1..sunk, s32[]{:T(128)} %constant.65.clone.1..sunk) | dynamic-update-slice | bytes 1048580 | tf_op jit(solution)/shard_map/while/body/jit(dynamic_update_index_in_dim)/dynamic_update_slice | solution.py:137
  504.7 132.2 %all-gather.2 = bf16[64,1,16]{2,1,0:T(2,128)(2,1)S(1)} all-gather(bf16[1,1,16]{2,1,0:T(2,128)(2,1)S(1)} %bitcast.152), channel_id=1, replica_groups=mesh['seq'=64,'tp'=8] {'seq'}, dimensions={0}, use_global_device_ids=true | all-gather | bytes 2080 | tf_op jit(solution)/shard_map/all_gather | solution.py:30
  637.3 2.1 reshape.118
  639.3 286.3 %all-gather.11.cloned.1.call-done = bf16[1024,64,128]{2,1,0:T(8,128)(2,1)} async-done(((bf16[16,64,128]{2,1,0:T(8,128)(2,1)}), bf16[1024,64,128]{2,1,0:T(8,128)(2,1)}) %all-gather.11.cloned.1.call-update) | async-done | bytes 16777232 | tf_op jit(solution)/shard_map/all_gather | solution.py:30
  925.6 73.0 %while.30 = (s32[]{:T(128)}, f32[16]{0:T(128)S(1)}, f32[16,64,128]{2,1,0:T(8,128)S(1)}, s32[]{:T(128)}, bf16[64,16]{1,0:T(8,128)(2,1)S(1)}, /*index=5*/bf16[64,16,64,128]{3,2,1,0:T(8,128)(2,1)}, s32[]{:T(128)}, s32[]{:T(128)}) while((s32[]{:T(128)}, f32[16]{0:T(128)S(1)}, f32[16,64,128]{2,1,0:T(8,128)S(1)}, s32[]{:T(128)}, ...), condition=%wide.region_6.7_spmd.clone, body=%wide.region_5.6_spmd.clone.sunk | while | flops 655428 | bytes 1311123 | solution.py:43
  925.7 1.1 fusion.85
  928.0 1.1 fusion.85
  929.1 1.1 fusion.85
  931.4 1.1 fusion.85
  932.5 1.1 fusion.85
  934.8 1.1 fusion.85
  936.0 1.1 fusion.85
  939.4 1.1 fusion.85
  1000.1 14.5 %psum.7 = f32[256]{0:T(256)S(1)} all-reduce(f32[256]{0:T(256)S(1)} %get-tuple-element.306), channel_id=1, replica_groups=mesh['seq'=64,'tp'=8] {'tp'}, use_global_device_ids=true, to_apply=%region_9.10 | all-reduce | flops 256 | bytes 2048 | tf_op jit(solution)/shard_map/psum | solution.py:159
  (220 shorter events, 76.1 us)
Async XLA Ops:
  11.7 16.6 %copy-start.5 = (bf16[64,32]{0,1:T(8,128)(2,1)S(1)}, bf16[64,32]{0,1:T(8,128)(2,1)}, u32[]{:S(2)}) copy-start(bf16[64,32]{0,1:T(8,128)(2,1)} %param.18) | copy-start | bytes 12292
  11.7 175.2 %copy-start.6 = (bf16[64,16]{0,1:T(8,128)(2,1)S(1)}, bf16[64,16]{0,1:T(8,128)(2,1)}, u32[]{:S(2)}) copy-start(bf16[64,16]{0,1:T(8,128)(2,1)} %param.19) | copy-start | bytes 6148
  11.7 312.3 %copy-start.7 = (f32[4,256]{1,0:T(4,128)S(1)}, f32[4,256]{1,0:T(4,128)}, u32[]{:S(2)}) copy-start(f32[4,256]{1,0:T(4,128)} %param.21) | copy-start | bytes 12292
  11.7 312.3 %copy-start.4 = (f32[4,1024]{1,0:T(4,128)S(1)}, f32[4,1024]{1,0:T(4,128)}, u32[]{:S(2)}) copy-start(f32[4,1024]{1,0:T(4,128)} %param.20) | copy-start | bytes 49156
  11.8 449.8 %all-to-all-start = ((bf16[64,64,1024]{2,1,0:T(8,128)(2,1)}), bf16[64,64,1024]{2,1,0:T(8,128)(2,1)}, u32[]{:S(2)}, u32[]{:S(2)}) async-start(bf16[64,64,1024]{2,1,0:T(8,128)(2,1)} %stack.2), calls=%async_computation | async-start | bytes 16777216 | tf_op jit(solution)/shard_map/all_to_all | solution.py:14
  27.5 296.6 %all-gather.7.cloned.1.call-start = ((), (), s32[]{:S(2)}) async-start(), calls=%async_computation.1 | async-start | bytes 2359296 | tf_op jit(solution)/shard_map/all_gather | solution.py:95
  28.2 430.3 %all-gather.9.cloned.1.call-start = ((), (), s32[]{:S(2)}) async-start(), calls=%async_computation.2 | async-start | bytes 2129920 | tf_op jit(solution)/shard_map/all_gather | solution.py:105
  186.9 738.8 %all-gather.11.cloned.1.call-start = ((), (), s32[]{:S(2)}) async-start(), calls=%async_computation.3 | async-start | bytes 17039360 | tf_op jit(solution)/shard_map/all_gather | solution.py:30
  324.1 137.5 %copy-start = (bf16[256,4096]{1,0:T(8,128)(2,1)S(1)}, bf16[256,4096]{1,0:T(8,128)(2,1)}, u32[]{:S(2)}) copy-start(bf16[256,4096]{1,0:T(8,128)(2,1)} %all-gather.7.cloned.1.call-done) | copy-start | bytes 6291460
  461.6 7.8 copy-start.8
  461.6 7.8 copy-start.10
  467.3 2.9 collective-permute-start
  472.7 30.8 %copy-start.3 = (f32[1024]{0:T(1024)S(1)}, f32[1024]{0:T(1024)}, u32[]{:S(2)}) copy-start(f32[1024]{0:T(1024)} %param.25) | copy-start | bytes 12292
  472.7 30.8 %copy-start.2 = (f32[1024]{0:T(1024)S(1)}, f32[1024]{0:T(1024)}, u32[]{:S(2)}) copy-start(f32[1024]{0:T(1024)} %param.27) | copy-start | bytes 12292
  925.6 73.0 %copy-start.1 = (f32[16,64,128]{2,1,0:T(8,128)S(1)}, f32[16,64,128]{2,1,0:T(8,128)}, u32[]{:S(2)}) copy-start(f32[16,64,128]{2,1,0:T(8,128)} %param.26) | copy-start | bytes 1572868
  925.6 73.0 %copy-start.9 = (f32[16]{0:T(128)S(1)}, f32[16]{0:T(128)}, u32[]{:S(2)}) copy-start(f32[16]{0:T(128)} %param.24) | copy-start | bytes 196
Sparse Core Ops, SparseCore 0:
  30.5 47.6 all-gather.6
  187.0 271.5 all-gather.8
  503.6 422.0 all-gather.10
